TPU v7x, 32 devices: a whole 2x2x4 slice. The times are simulated.
32 devices in a mesh: group: 2 (over y), ctx: 4 (over x, core), tp: 4 (over z).
Axes of the slice: x: 2, y: 2, z: 4, core: 2. Of those that a mesh axis runs over, the one named last changes fastest.
Arguments:
- tokens: bfloat16 [1024, 5376], P(('group', 'ctx'), 'tp'), parts along dimension 0
- positions: int32 [1024], P(('group', 'ctx')), parts along dimension 0, may hold values from 0 to 383, as said below
- first_key: int32 [1024], P(('group', 'ctx')), parts along dimension 0, may hold values from 0 to 511, as said below
- input_gain: float32 [5376], replicated, may hold values from 0.1 to 1.9
- query_weight: bfloat16 [5376, 4096], P(None, 'tp'), may hold values from -0.078125 to 0.078125
- kv_weight: bfloat16 [2, 5376, 2048], P(None, None, 'tp'), may hold values from -0.078125 to 0.078125
- query_gain: float32 [128], replicated, may hold values from 0.1 to 1.9
- key_gain: float32 [128], replicated, may hold values from 0.1 to 1.9
- out_weight: bfloat16 [4096, 5376], P('tp'), may hold values from -0.125 to 0.125
- post_gain: float32 [5376], replicated, may hold values from 0.1 to 1.9
Outputs:
- layer_out: bfloat16 [1024, 5376], P(('group', 'ctx'), 'tp'), parts along dimension 0
There are 2 independent parts, one for each index of `group`. A program takes and returns all parts, laid end to end along the dimension named above; an argument that names none is the same for every part. Nothing has to cross between parts.
Inputs may be any that keep to these rules, and one draw needn't show every extreme that they name: `positions`: A token's position is its offset within its document. Documents are contiguous runs of tokens; exactly one of them is 384 tokens long, every other one is shorter, and the last token forms a document of its own. first_key[i] is the larger of i - 1023 and the index of the first token of i's document (documents as described for positions).
All inputs are finite; a program needn't handle non-finite values.
Results may differ from a plain program's by a relative error of at most 0.014.
Values may be sent and summed in bfloat16 or wider, within the bound.
A program may use at most 128 MiB of HBM per device.

v0:
```python
import math

import jax
import jax.numpy as jnp
from jax import lax
from jax.sharding import PartitionSpec as P

D = 5376
H = 32
WINDOW = 1024


EPSILON = 1e-06


def from_partner(array, axis, distance):
    return lax.ppermute(array, axis, [(i, i ^ 1 << distance) for i in range(lax.axis_size(axis))])


def passed_along(block, axis, distance):
    devices = range(lax.axis_size(axis))
    route = [(i - distance, i) for i in devices if i - distance in devices]
    return lax.ppermute(block, axis, route)


def rms_norm(values, gain_vec):
    return (
        values * lax.rsqrt(jnp.mean(values * values, axis=-1, keepdims=True) + EPSILON) * gain_vec
    )


def rotate(values, positions_in):
    half_dim = values.shape[-1] // 2
    frequency = jnp.exp(
        jnp.arange(half_dim, dtype=jnp.float32) * (-2.0 * math.log(10000.0) / values.shape[-1])
    )
    angles = positions_in.astype(jnp.float32)[:, None] * frequency[None, :]
    cosines = jnp.cos(angles)[:, None, :]
    sine_part = jnp.sin(angles)[:, None, :]
    lower_half = values[..., :half_dim]
    upper_half = values[..., half_dim:]
    return jnp.concatenate(
        [
            lower_half * cosines - upper_half * sine_part,
            upper_half * cosines + lower_half * sine_part,
        ],
        axis=-1,
    )


def per_device(
    tokens,
    positions,
    first_key,
    input_gain,
    query_weight,
    kv_weight,
    query_gain,
    key_gain,
    out_weight,
    post_gain,
):
    tok_rows = tokens.shape[0]
    feat_dev = tokens.shape[1]
    head_dim = query_gain.shape[0]
    heads_dev = query_weight.shape[1] // head_dim
    tp_index = lax.axis_index("tp")
    ctx_index = lax.axis_index("ctx")
    ctx_count = lax.axis_size("ctx")
    local_x = tokens.astype(jnp.float32)
    kv_full = kv_weight
    if heads_dev == 1:
        partner = from_partner(kv_weight, "tp", 0)
        is_even = tp_index % 2 == 0
        kv_full = jnp.where(
            is_even,
            jnp.concatenate([kv_weight, partner], axis=2),
            jnp.concatenate([partner, kv_weight], axis=2),
        )
    gathered = lax.all_gather(tokens, "tp", axis=1, tiled=True).astype(jnp.float32)
    normed = rms_norm(gathered, input_gain).astype(jnp.bfloat16)
    query_raw = jnp.dot(normed, query_weight, preferred_element_type=jnp.float32)
    key_raw = jnp.dot(normed, kv_full[0], preferred_element_type=jnp.float32)
    value_raw = jnp.dot(normed, kv_full[1], preferred_element_type=jnp.float32)
    kv_heads = key_raw.shape[1] // head_dim
    group_size = heads_dev // kv_heads
    queries = (
        rotate(rms_norm(query_raw.reshape(tok_rows, heads_dev, head_dim), query_gain), positions)
        * (D // H) ** (-0.5)
    ).astype(jnp.bfloat16)
    keys = rotate(
        rms_norm(key_raw.reshape(tok_rows, kv_heads, head_dim), key_gain), positions
    ).astype(jnp.bfloat16)
    values_b = value_raw.reshape(tok_rows, kv_heads, head_dim).astype(jnp.bfloat16)
    kv_block = jnp.stack([keys, values_b])
    reach_blocks = min(ctx_count - 1, (WINDOW + tok_rows - 2) // tok_rows)
    received = []
    moving = kv_block
    for offset in range(reach_blocks):
        moving = passed_along(moving, "ctx", 1)
        received.append(moving)
    blocks = received[::-1] + [kv_block]
    keys_all = jnp.concatenate(blocks, axis=1)
    key_count = keys_all.shape[1]
    key_index = (ctx_index - reach_blocks) * tok_rows + jnp.arange(key_count, dtype=jnp.int32)
    query_index = ctx_index * tok_rows + jnp.arange(tok_rows, dtype=jnp.int32)
    visible = (key_index[None, :] >= first_key[:, None]) & (
        key_index[None, :] <= query_index[:, None]
    )
    grouped = queries.reshape(tok_rows, kv_heads, group_size, head_dim)
    scores = jnp.einsum("qkgd,tkd->kgqt", grouped, keys_all[0], preferred_element_type=jnp.float32)
    scores = jnp.where(visible[None, None], scores, -1e30)
    row_max = jnp.max(scores, axis=-1, keepdims=True)
    weights = jnp.exp(scores - row_max)
    denominator = jnp.sum(weights, axis=-1)
    mixed_out = jnp.einsum(
        "kgqt,tkd->qkgd",
        weights.astype(jnp.bfloat16),
        keys_all[1],
        preferred_element_type=jnp.float32,
    )
    mixed_out = mixed_out / jnp.transpose(denominator, (2, 0, 1))[..., None]
    attn = mixed_out.astype(jnp.bfloat16).reshape(tok_rows, heads_dev * head_dim)
    partial_value = jnp.dot(attn, out_weight, preferred_element_type=jnp.float32)
    summed = lax.psum(partial_value.astype(jnp.bfloat16), "tp").astype(jnp.float32)
    post_normed = rms_norm(summed, post_gain)
    own_cols = lax.dynamic_slice_in_dim(post_normed, tp_index * feat_dev, feat_dev, 1)
    return (local_x + own_cols).astype(jnp.bfloat16)


def solution(mesh):
    return jax.shard_map(
        per_device,
        mesh=mesh,
        in_specs=(
            P(("group", "ctx"), "tp"),
            P(("group", "ctx")),
            P(("group", "ctx")),
            P(),
            P(None, "tp"),
            P(None, None, "tp"),
            P(),
            P(),
            P("tp", None),
            P(),
        ),
        out_specs=P(("group", "ctx"), "tp"),
        check_vma=False,
    )
```

profile of v0, /device:TPU:2, one launch (start us, length us, event | category | flops | bytes accessed | tf_op | source)
XLA Modules:
  0.0 160.8 jit_solution(8768444792018409563)
XLA Ops:
  6.5 0.7 all-gather.2.cloned.1.call-update
  7.3 8.9 %slice_bitcast_fusion.1 = (bf16[512,5376]{0,1:T(8,128)(2,1)}, bf16[512,5376]{0,1:T(8,128)(2,1)}) fusion(bf16[2,5376,512]{2,1,0:T(8,128)(2,1)} %param.15), kind=kLoop, calls=%fused_computation.2 | loop fusion | bytes 22020096 | tf_op jit(solution)/shard_map/dot_general | solution.py:83
  16.3 8.5 %copy.37 = bf16[512,5376]{1,0:T(8,128)(2,1)} copy(bf16[512,5376]{0,1:T(8,128)(2,1)} %get-tuple-element.5) | data formatting | bytes 11010048 | tf_op jit(solution)/shard_map/dot_general | solution.py:83
  24.7 8.3 %copy.39 = bf16[512,5376]{1,0:T(8,128)(2,1)} copy(bf16[512,5376]{0,1:T(8,128)(2,1)} %get-tuple-element.6) | data formatting | bytes 11010048 | tf_op jit(solution)/shard_map/dot_general | solution.py:84
  33.0 0.2 multiply_cosine_fusion
  33.5 0.1 compare_and_fusion
  33.6 10.2 %all-gather.2.cloned.1.call-done = bf16[128,5376]{0,1:T(8,128)(2,1)} async-done(((bf16[128,1344]{0,1:T(8,128)(2,1)}), bf16[128,5376]{0,1:T(8,128)(2,1)}) %all-gather.2.cloned.1.call-update) | async-done | bytes 1376272 | tf_op jit(solution)/shard_map/all_gather | solution.py:80
  43.8 2.1 %fusion = f32[128]{0:T(128)S(1)} fusion(bf16[128,5376]{0,1:T(8,128)(2,1)} %all-gather.2.cloned.1.call-done), kind=kLoop, calls=%fused_computation.5 | loop fusion | flops 2064256 | bytes 1376768 | tf_op jit(solution)/shard_map/reduce_sum | solution.py:28
  45.9 4.8 %multiply_reduce_fusion.2 = (f32[128,4]{0,1:T(4,128)S(1)}, f32[128,4,128]{0,2,1:T(8,128)S(1)}) fusion(bf16[4,128,5376]{2,1,0:T(8,128)(2,1)} %bitcast.74, f32[5376]{0:T(1024)S(1)} %copy-done.4, f32[128]{0:T(128)S(1)} %add_rsqrt_fusion.3, bf16[128,5376]{0,1:T(8,128)(2,1)} %all-gather.2.cloned.1.call-done), kind=kOutput, calls=%fused_computation.44 | convolution fusion | flops 707526144 | bytes 7167488 | tf_op jit(solution)/shard_map/dot_general | solution.py:83
  50.9 1.7 %fusion.15 = bf16[1,128,4,128]{1,3,2,0:T(8,128)(2,1)S(1)} fusion(bf16[4,128,5376]{2,1,0:T(8,128)(2,1)S(1)} %bitcast.73, bf16[128,5376]{0,1:T(8,128)(2,1)S(1)} %copy-done, f32[5376]{0:T(1024)S(1)} %copy-done.4, f32[128]{0:T(128)S(1)} %add_rsqrt_fusion.3), kind=kOutput, calls=%fused_computation.23 | convolution fusion | flops 707461120 | bytes 7034368 | tf_op jit(solution)/shard_map/dot_general | solution.py:84
  52.7 1.9 %collective-permute-start = (bf16[2,128,4,128]{1,3,2,0:T(8,128)(2,1)S(1)}, bf16[2,128,4,128]{1,3,2,0:T(8,128)(2,1)S(1)}, u32[]{:S(2)}, u32[]{:S(2)}) collective-permute-start(bf16[2,128,4,128]{1,3,2,0:T(8,128)(2,1)S(1)} %pad_maximum_fusion), channel_id=1, source_target_pairs={{0,4},{4,8},{8,12},{1,5},{5,9},{9,13},{2,6},{6,10},{10,14},{3,7},{... | collective-permute-start | bytes 786440 | tf_op jit(solution)/shard_map/ppermute | solution.py:23
  54.6 6.4 %convolution_bitcast_fusion.1 = f32[16,8,8,128]{3,1,2,0:T(8,128)S(1)} fusion(bf16[5376,1024]{1,0:T(8,128)(2,1)} %param.14, bf16[128,5376]{0,1:T(8,128)(2,1)S(1)} %copy-done, f32[5376]{0:T(1024)S(1)} %copy-done.4, f32[128]{0:T(128)S(1)} %add_rsqrt_fusion.3), kind=kOutput, calls=%fused_computation.20 | convolution fusion | flops 1412038656 | bytes 12932608 | tf_op jit(solution)/shard_map/dot_general | solution.py:82
  61.2 0.2 multiply_reduce_fusion.1
  61.4 1.9 %collective-permute-start.1 = (bf16[2,128,4,128]{1,3,2,0:T(8,128)(2,1)S(1)}, bf16[2,128,4,128]{1,3,2,0:T(8,128)(2,1)S(1)}, u32[]{:S(2)}, u32[]{:S(2)}) collective-permute-start(bf16[2,128,4,128]{1,3,2,0:T(8,128)(2,1)S(1)} %collective-permute-done), channel_id=1, source_target_pairs={{0,4},{4,8},{8,12},{1,5},{5,9},{9,13},{2,6},{6,10},{10,14},{3,7},{... | collective-permute-start | bytes 786440 | tf_op jit(solution)/shard_map/ppermute | solution.py:23
  63.5 0.2 multiply_multiply_fusion
  63.7 5.4 %collective-permute-done.1 = bf16[2,128,4,128]{1,3,2,0:T(8,128)(2,1)S(1)} collective-permute-done((bf16[2,128,4,128]{1,3,2,0:T(8,128)(2,1)S(1)}, bf16[2,128,4,128]{1,3,2,0:T(8,128)(2,1)S(1)}, u32[]{:S(2)}, u32[]{:S(2)}) %collective-permute-start.1) | collective-permute-done | bytes 262176 | tf_op jit(solution)/shard_map/ppermute | solution.py:23
  69.1 2.1 %collective-permute-start.2 = (bf16[2,128,4,128]{1,3,2,0:T(8,128)(2,1)S(1)}, bf16[2,128,4,128]{1,3,2,0:T(8,128)(2,1)S(1)}, u32[]{:S(2)}, u32[]{:S(2)}) collective-permute-start(bf16[2,128,4,128]{1,3,2,0:T(8,128)(2,1)S(1)} %collective-permute-done.1), channel_id=1, source_target_pairs={{0,4},{4,8},{8,12},{1,5},{5,9},{9,13},{2,6},{6,10},{10,14},{3,7},{... | collective-permute-start | bytes 786440 | tf_op jit(solution)/shard_map/ppermute | solution.py:23
  71.2 0.3 multiply_subtract_fusion
  71.5 0.1 copy.46
  71.6 0.1 copy.47
  71.7 5.1 %collective-permute-done.2 = bf16[2,128,4,128]{1,3,2,0:T(8,128)(2,1)S(1)} collective-permute-done((bf16[2,128,4,128]{1,3,2,0:T(8,128)(2,1)S(1)}, bf16[2,128,4,128]{1,3,2,0:T(8,128)(2,1)S(1)}, u32[]{:S(2)}, u32[]{:S(2)}) %collective-permute-start.2) | collective-permute-done | bytes 262176 | tf_op jit(solution)/shard_map/ppermute | solution.py:23
  76.8 0.1 maximum_maximum_fusion
  76.9 0.6 fusion.3
  77.6 0.4 fusion.4
  78.0 0.6 fusion.11
  78.6 9.6 %convolution_convert_fusion = bf16[128,5376]{0,1:T(8,128)(2,1)} fusion(bf16[128,1024]{0,1:T(8,128)(2,1)S(1)} %bitcast.78, bf16[1024,5376]{1,0:T(8,128)(2,1)} %param.18), kind=kOutput, calls=%fused_computation | convolution fusion | flops 1409974272 | bytes 12648448 | tf_op jit(solution)/shard_map/dot_general | solution.py:124
  88.2 0.8 dynamic-slice
  89.0 60.8 %all-reduce.2.cloned.1.call-done = bf16[128,5376]{0,1:T(8,128)(2,1)} async-done(((bf16[128,5376]{0,1:T(8,128)(2,1)}), bf16[128,5376]{0,1:T(8,128)(2,1)}) %all-reduce.2.cloned.1.call-update) | async-done | bytes 1376272 | tf_op jit(solution)/shard_map/psum | solution.py:125
  149.8 2.2 %multiply_reduce_fusion = f32[128]{0:T(128)S(1)} fusion(bf16[128,5376]{0,1:T(8,128)(2,1)} %all-reduce.2.cloned.1.call-done), kind=kLoop, calls=%fused_computation.8 | loop fusion | flops 2064256 | bytes 1376768 | tf_op jit(solution)/shard_map/reduce_sum | solution.py:28
  152.0 0.2 convert_element_type.52
  152.2 0.8 copy-done.3
  153.0 1.0 fusion.24
  (37 shorter events, 0.7 us)
Async XLA Ops:
  6.5 37.3 %all-gather.2.cloned.1.call-start = ((), (), s32[]{:S(2)}) async-start(), calls=%async_computation | async-start | bytes 1720320 | tf_op jit(solution)/shard_map/all_gather | solution.py:80
  7.3 142.6 %all-reduce.2.cloned.1.call-start = ((), (), s32[]{:S(2)}) async-start(), calls=%async_computation.1 | async-start | bytes 2752512 | tf_op jit(solution)/shard_map/psum | solution.py:125
  16.3 8.5 %copy-start.8 = (s32[128]{0:T(128)S(1)}, s32[128]{0:T(128)}, u32[]{:S(2)}) copy-start(s32[128]{0:T(128)} %param.11) | copy-start | bytes 1540
  24.7 8.7 %copy-start.5 = (s32[128]{0:T(128)S(1)}, s32[128]{0:T(128)}, u32[]{:S(2)}) copy-start(s32[128]{0:T(128)} %param.12) | copy-start | bytes 1540
  24.7 21.1 %copy-start.4 = (f32[5376]{0:T(1024)S(1)}, f32[5376]{0:T(1024)}, u32[]{:S(2)}) copy-start(f32[5376]{0:T(1024)} %param.13) | copy-start | bytes 64516
  45.9 4.9 %copy-start.6 = (f32[128]{0:T(128)S(1)}, f32[128]{0:T(128)}, u32[]{:S(2)}) copy-start(f32[128]{0:T(128)} %param.17) | copy-start | bytes 1540
  45.9 5.0 %copy-start = (bf16[128,5376]{0,1:T(8,128)(2,1)S(1)}, bf16[128,5376]{0,1:T(8,128)(2,1)}, u32[]{:S(2)}) copy-start(bf16[128,5376]{0,1:T(8,128)(2,1)} %all-gather.2.cloned.1.call-done) | copy-start | bytes 4128772
  45.9 5.0 %copy-start.1 = (bf16[512,5376]{1,0:T(8,128)(2,1)S(1)}, bf16[512,5376]{1,0:T(8,128)(2,1)}, u32[]{:S(2)}) copy-start(bf16[512,5376]{1,0:T(8,128)(2,1)} %copy.39) | copy-start | bytes 16515076
  52.7 10.8 %copy-start.7 = (f32[128]{0:T(128)S(1)}, f32[128]{0:T(128)}, u32[]{:S(2)}) copy-start(f32[128]{0:T(128)} %param.16) | copy-start | bytes 1540
  52.7 8.7 %collective-permute-start = (bf16[2,128,4,128]{1,3,2,0:T(8,128)(2,1)S(1)}, bf16[2,128,4,128]{1,3,2,0:T(8,128)(2,1)S(1)}, u32[]{:S(2)}, u32[]{:S(2)}) collective-permute-start(bf16[2,128,4,128]{1,3,2,0:T(8,128)(2,1)S(1)} %pad_maximum_fusion), channel_id=1, source_target_pairs={{0,4},{4,8},{8,12},{1,5},{5,9},{9,13},{2,6},{6,10},{10,14},{3,7},{... | collective-permute-start | bytes 786440 | tf_op jit(solution)/shard_map/ppermute | solution.py:23
  61.4 7.7 %collective-permute-start.1 = (bf16[2,128,4,128]{1,3,2,0:T(8,128)(2,1)S(1)}, bf16[2,128,4,128]{1,3,2,0:T(8,128)(2,1)S(1)}, u32[]{:S(2)}, u32[]{:S(2)}) collective-permute-start(bf16[2,128,4,128]{1,3,2,0:T(8,128)(2,1)S(1)} %collective-permute-done), channel_id=1, source_target_pairs={{0,4},{4,8},{8,12},{1,5},{5,9},{9,13},{2,6},{6,10},{10,14},{3,7},{... | collective-permute-start | bytes 786440 | tf_op jit(solution)/shard_map/ppermute | solution.py:23
  69.1 7.7 %collective-permute-start.2 = (bf16[2,128,4,128]{1,3,2,0:T(8,128)(2,1)S(1)}, bf16[2,128,4,128]{1,3,2,0:T(8,128)(2,1)S(1)}, u32[]{:S(2)}, u32[]{:S(2)}) collective-permute-start(bf16[2,128,4,128]{1,3,2,0:T(8,128)(2,1)S(1)} %collective-permute-done.1), channel_id=1, source_target_pairs={{0,4},{4,8},{8,12},{1,5},{5,9},{9,13},{2,6},{6,10},{10,14},{3,7},{... | collective-permute-start | bytes 786440 | tf_op jit(solution)/shard_map/ppermute | solution.py:23
  149.8 2.2 %copy-start.2 = (bf16[128,5376]{0,1:T(8,128)(2,1)S(1)}, bf16[128,5376]{0,1:T(8,128)(2,1)}, u32[]{:S(2)}) copy-start(bf16[128,5376]{0,1:T(8,128)(2,1)} %all-reduce.2.cloned.1.call-done) | copy-start | bytes 4128772
  152.0 1.0 copy-start.3
Sparse Core Ops, SparseCore 0:
  8.9 34.8 all-gather.1
  88.3 61.4 all-reduce.1
where the time goes:
time: 163 us; the launch traced here: 161 us
  waiting for transfers between devices  82.3 us (50%)
  local copies, waits for them, and re-layouts  27.9 us (17%)
  matrix products  23.8 us (15%)
  between operations  13.7 us (8%)
  other arithmetic  7.11 us (4%)
  starting transfers between devices  5.98 us (4%)
    psum x1, waiting for transfers between devices, per_device(): lax.psum(partial_value.astype(jnp.bfloat16), 'tp').astype(jnp.float32)  60.8 us
    dot_general x2, local copies, waits for them, and re-layouts, per_device(): key_raw = jnp.dot(normed, kv_full[0], preferred_element_type=jnp.float32)  17.4 us
    ppermute x3, waiting for transfers between devices, passed_along(): return lax.ppermute(block, axis, route)  10.5 us
    all_gather x1, waiting for transfers between devices, per_device(): lax.all_gather(tokens, 'tp', axis=1, tiled=True).astype(jnp.float32)  10.2 us
    dot_general x1, matrix products, per_device(): jnp.dot(attn, out_weight, preferred_element_type=jnp.float32)  9.61 us
    dot_general x1, local copies, waits for them, and re-layouts, per_device(): value_raw = jnp.dot(normed, kv_full[1], preferred_element_type=jnp.float32)  8.27 us
    dot_general x1, matrix products, per_device(): jnp.dot(normed, query_weight, preferred_element_type=jnp.float32)  6.44 us
    ppermute x3, starting transfers between devices, passed_along(): return lax.ppermute(block, axis, route)  5.94 us
  transfers between devices with their start and end apart: 5, of which 4 were waited for; matrix products, arithmetic and copies ran while one was open for 22% of the time, Pallas kernels for 0%

commit v1 on v0

--- a/solution.py
+++ b/solution.py
@@ -3,6 +3,8 @@
 import jax
 import jax.numpy as jnp
 from jax import lax
+from jax.experimental import pallas as pl
+from jax.experimental.pallas import tpu as pltpu
 from jax.sharding import PartitionSpec as P
 
 D = 5376
@@ -128,9 +130,492 @@
     return (local_x + own_cols).astype(jnp.bfloat16)
 
 
+MESH = pl.DeviceIdType.MESH
+F32 = jnp.float32
+BF16 = jnp.bfloat16
+TP = 4
+CTX = 4
+CHUNKS = 2
+PRESCALE = 2.0**-10
+
+
+def fused_kernel(
+    tok_ref, pos_ref, fk_ref, ig_ref, qg_ref, kg_ref, pg_ref, qw_hbm, kvw_hbm, ow_hbm, out_ref,
+    xbuf, xg_ref, wq, wkv, wo, gain_in, gain_post, ssq_ref, kv_acc, q_acc, cos_ref, sin_ref,
+    kvbuf, q_ref, m_ref, l_ref, o_ref, attn_ref, part, rup, rdn, own, sq_mine, sq_all,
+    w_sem, wo_sem, ag_up, ag_dn, ag_recv, kv_send, kv_recv,
+    rs_up_send, rs_dn_send, rs_up_recv, rs_dn_recv, sq_send, sq_recv,
+):
+    rows, feat = tok_ref.shape
+    hd = qg_ref.shape[1]
+    kv_heads = wkv.shape[2] // hd
+    heads = wq.shape[1] // hd
+    model = feat * TP
+    z = lax.axis_index("tp")
+    c = lax.axis_index("ctx")
+    partner = c + 1 - 2 * (c % 2)
+    far = lax.rem(c + 2, CTX)
+    crow = rows // CHUNKS
+    ch_rows = [pl.ds(i * crow, crow) for i in range(CHUNKS)]
+
+    def weight_copies(src):
+        span = pl.ds(pl.multiple_of(src * feat, 64), feat)
+        return (
+            pltpu.make_async_copy(kvw_hbm.at[0, span], wkv.at[0, span], w_sem.at[src, 0]),
+            pltpu.make_async_copy(kvw_hbm.at[1, span], wkv.at[1, span], w_sem.at[src, 1]),
+            pltpu.make_async_copy(qw_hbm.at[span], wq.at[span], w_sem.at[src, 2]),
+        )
+
+    def each_source(fn):
+        def at_distance(d, carry):
+            @pl.when(z - d >= 0)
+            def _():
+                fn(z - d, d)
+
+            @pl.when((z + d < TP) & (d > 0))
+            def _():
+                fn(z + d, d)
+
+            return carry
+
+        lax.fori_loop(0, TP, at_distance, 0)
+
+    def begin_weights(src, d):
+        for copy in weight_copies(src):
+            copy.start()
+
+    each_source(begin_weights)
+    wo_copy = pltpu.make_async_copy(ow_hbm, wo, wo_sem)
+    wo_copy.start()
+
+    barrier = pltpu.get_barrier_semaphore()
+    for d in range(1, TP):
+        pl.semaphore_signal(
+            barrier, inc=1, device_id={"tp": lax.rem(z + d, TP)}, device_id_type=MESH
+        )
+    pl.semaphore_signal(barrier, inc=1, device_id={"ctx": partner}, device_id_type=MESH)
+    pl.semaphore_signal(barrier, inc=1, device_id={"ctx": far}, device_id_type=MESH)
+    pl.semaphore_wait(barrier, TP + 1)
+
+    up = {"tp": lax.rem(z + 1, TP)}
+    down = {"tp": lax.rem(z + TP - 1, TP)}
+
+    def ag_copy(source, src, ch, send, target):
+        return pltpu.make_async_remote_copy(
+            src_ref=source,
+            dst_ref=xbuf.at[src, ch_rows[ch]],
+            send_sem=send.at[src, ch],
+            recv_sem=ag_recv.at[src, ch],
+            device_id=target,
+            device_id_type=MESH,
+        )
+
+    for ch in range(CHUNKS):
+        @pl.when(z < TP - 1)
+        def _():
+            ag_copy(tok_ref.at[ch_rows[ch]], z, ch, ag_up, up).start()
+
+        @pl.when(z > 0)
+        def _():
+            ag_copy(tok_ref.at[ch_rows[ch]], z, ch, ag_dn, down).start()
+
+    for i in range(TP):
+        gain_in[i] = ig_ref[:, i * feat : (i + 1) * feat] * PRESCALE
+        gain_post[i] = pg_ref[:, i * feat : (i + 1) * feat]
+    xbuf[z] = tok_ref[...]
+    ssq_ref[...] = jnp.zeros_like(ssq_ref)
+    kv_acc[...] = jnp.zeros_like(kv_acc)
+    q_acc[...] = jnp.zeros_like(q_acc)
+    r_iota = lax.broadcasted_iota(jnp.int32, (rows, rows), 0)
+    c_iota = lax.broadcasted_iota(jnp.int32, (rows, rows), 1)
+    diagonal = r_iota == c_iota
+
+    def as_column(row):
+        return jnp.sum(jnp.where(diagonal, row, 0.0), axis=1, keepdims=True)
+
+    lane = lax.broadcasted_iota(jnp.int32, (rows, hd), 1)
+    half = jnp.where(lane < hd // 2, lane, lane - hd // 2).astype(F32)
+    angles = as_column(pos_ref[...].astype(F32)) * jnp.exp(half * (-2.0 * math.log(10000.0) / hd))
+    cos_ref[...] = jnp.cos(angles)
+    sines = jnp.sin(angles)
+    sin_ref[...] = jnp.where(lane < hd // 2, -sines, sines)
+    first = as_column(fk_ref[...].astype(F32)).astype(jnp.int32)
+
+    last = jnp.where(z < TP // 2, TP - 1, 0)
+
+    def query_product(src):
+        span = pl.ds(pl.multiple_of(src * feat, 64), feat)
+        weight_copies(src)[2].wait()
+        q_acc[...] += jnp.dot(xg_ref[...], wq[span], preferred_element_type=F32)
+
+    def projections(src):
+        x = xbuf[src].astype(F32)
+        ssq_ref[...] += jnp.sum(x * x, axis=1, keepdims=True)
+        xg_ref[...] = (x * gain_in[src]).astype(BF16)
+        span = pl.ds(pl.multiple_of(src * feat, 64), feat)
+        width = wkv.shape[2]
+        for i in range(2):
+            weight_copies(src)[i].wait()
+            kv_acc[:, i * width : (i + 1) * width] += jnp.dot(
+                xg_ref[...], wkv[i, span], preferred_element_type=F32
+            )
+
+        @pl.when(src != last)
+        def _():
+            query_product(src)
+
+    def at_distance(d, carry):
+        low = z - d
+        high = z + d
+        for ch in range(CHUNKS):
+            @pl.when((d > 0) & (low >= 0))
+            def _():
+                here = xbuf.at[low, ch_rows[ch]]
+                ag_copy(here, low, ch, ag_up, down).wait_recv()
+
+                @pl.when(z < TP - 1)
+                def _():
+                    ag_copy(here, low, ch, ag_up, up).start()
+
+            @pl.when((d > 0) & (high < TP))
+            def _():
+                here = xbuf.at[high, ch_rows[ch]]
+                ag_copy(here, high, ch, ag_dn, up).wait_recv()
+
+                @pl.when(z > 0)
+                def _():
+                    ag_copy(here, high, ch, ag_dn, down).start()
+
+        def side(i, inner):
+            src = jnp.where(i == 0, low, high)
+
+            @pl.when((src >= 0) & (src < TP) & ((d > 0) | (i == 0)))
+            def _():
+                projections(src)
+
+            return inner
+
+        lax.fori_loop(0, 2, side, 0)
+        return carry
+
+    lax.fori_loop(0, TP, at_distance, 0)
+
+    inv = lax.rsqrt(ssq_ref[...] * (1.0 / model) + EPSILON) * (1.0 / PRESCALE)
+
+    def normed_rotated(raw, gain_vec):
+        raw = raw * inv
+        scaled = raw * lax.rsqrt(jnp.mean(raw * raw, axis=1, keepdims=True) + EPSILON) * gain_vec
+        return scaled * cos_ref[...] + pltpu.roll(scaled, hd // 2, 1) * sin_ref[...]
+
+    width = kv_heads * hd
+    for h in range(kv_heads):
+        cols = slice(h * hd, (h + 1) * hd)
+        kvbuf[c, 0, :, cols] = normed_rotated(kv_acc[:, cols], kg_ref[...]).astype(BF16)
+    kvbuf[c, 1] = (kv_acc[:, width:] * inv).astype(BF16)
+
+    def kv_copy(block, step, target):
+        return pltpu.make_async_remote_copy(
+            src_ref=kvbuf.at[block],
+            dst_ref=kvbuf.at[block],
+            send_sem=kv_send.at[step],
+            recv_sem=kv_recv.at[step],
+            device_id={"ctx": target},
+            device_id_type=MESH,
+        )
+
+    @pl.when(c < CTX // 2)
+    def _():
+        kv_copy(c, 1, far).start()
+
+    @pl.when(c % 2 == 0)
+    def _():
+        kv_copy(c, 0, partner).start()
+
+    query_product(last)
+    for h in range(heads):
+        cols = slice(h * hd, (h + 1) * hd)
+        spot = slice((h % 2) * rows, (h % 2 + 1) * rows)
+        q_ref[h // 2, spot] = (
+            normed_rotated(q_acc[:, cols], qg_ref[...]) * (D // H) ** (-0.5)
+        ).astype(BF16)
+
+    m_ref[...] = jnp.full_like(m_ref, -1e30)
+    l_ref[...] = jnp.zeros_like(l_ref)
+    o_ref[...] = jnp.zeros_like(o_ref)
+
+    def attend(block):
+        key_index = block * rows + c_iota
+        visible = (key_index >= first) & (key_index <= c * rows + r_iota)
+        bias = jnp.where(visible, 0.0, -1e30)
+        bias = jnp.concatenate([bias, bias], axis=0)
+        for h in range(kv_heads):
+            cols = slice(h * hd, (h + 1) * hd)
+            s = lax.dot_general(
+                q_ref[h], kvbuf[block, 0, :, cols], (((1,), (1,)), ((), ())),
+                preferred_element_type=F32,
+            )
+            s = jnp.where(bias < 0.0, -1e30, s)
+            old = m_ref[h]
+            new = jnp.maximum(old, jnp.max(s, axis=1, keepdims=True))
+            fade = jnp.exp(old - new)
+            p = jnp.exp(s - new)
+            m_ref[h] = new
+            l_ref[h] = l_ref[h] * fade + jnp.sum(p, axis=1, keepdims=True)
+            o_ref[h] = o_ref[h] * fade + jnp.dot(
+                p.astype(BF16), kvbuf[block, 1, :, cols], preferred_element_type=F32
+            )
+
+    def attention_step(step, carry):
+        block = jnp.where(
+            step == 0, c, jnp.where(step == 1, c - 1, jnp.where(step == 2, c - 2, partner - 2))
+        )
+        valid = (step == 0) | ((step == 1) & (c % 2 == 1)) | ((step >= 2) & (c >= CTX // 2))
+
+        @pl.when(valid)
+        def _():
+            @pl.when(step > 0)
+            def _():
+                kv_copy(block, step - 1, partner).wait_recv()
+
+            @pl.when(step == 2)
+            def _():
+                kv_copy(block, 2, partner).start()
+
+            attend(block)
+
+        return carry
+
+    lax.fori_loop(0, CTX, attention_step, 0)
+
+    for h in range(heads):
+        spot = slice((h % 2) * rows, (h % 2 + 1) * rows)
+        attn_ref[:, h * hd : (h + 1) * hd] = (
+            o_ref[h // 2, spot] / l_ref[h // 2, spot]
+        ).astype(BF16)
+
+    wo_copy.wait()
+
+    def rs_copy(dest, ch, buf, send, recv, target):
+        return pltpu.make_async_remote_copy(
+            src_ref=part.at[dest, ch_rows[ch]],
+            dst_ref=buf.at[dest, ch_rows[ch]],
+            send_sem=send.at[dest, ch],
+            recv_sem=recv.at[dest, ch],
+            device_id=target,
+            device_id_type=MESH,
+        )
+
+    def rs_up(dest, ch):
+        return rs_copy(dest, ch, rup, rs_up_send, rs_up_recv, up)
+
+    def rs_dn(dest, ch):
+        return rs_copy(dest, ch, rdn, rs_dn_send, rs_dn_recv, down)
+
+    shift = feat % 128
+    wide = feat + shift
+
+    def out_step(k, carry):
+        outer = TP - 1 - k
+        inner = jnp.where(k == 0, 3, jnp.where(k == 1, 0, jnp.where(k == 2, 2, 1)))
+        edge = (z == 0) | (z == TP - 1)
+        dest = jnp.where(edge, outer, inner)
+        dest = jnp.where(z < TP // 2, dest, TP - 1 - dest)
+        odd = dest % 2
+        start = pl.multiple_of((dest // 2) * (2 * feat) + odd * (feat - shift), 128)
+        term = jnp.dot(
+            attn_ref[...], wo[:, pl.ds(start, wide)], preferred_element_type=F32
+        ).astype(BF16)
+
+        @pl.when(odd == 0)
+        def _():
+            part[dest] = term[:, :feat]
+
+        @pl.when(odd == 1)
+        def _():
+            part[dest] = term[:, shift:]
+
+        for ch in range(CHUNKS):
+            @pl.when((z == 0) & (dest > 0))
+            def _():
+                rs_up(dest, ch).start()
+
+            @pl.when((z == TP - 1) & (dest < TP - 1))
+            def _():
+                rs_dn(dest, ch).start()
+
+        return carry
+
+    lax.fori_loop(0, TP, out_step, 0)
+    own[...] = part[z].astype(F32)
+
+    def sum_step(k, carry):
+        for ch in range(CHUNKS):
+            span = ch_rows[ch]
+            for dest, has, onward, buf, copy in (
+                (TP - 1 - k, (z > 0) & (TP - 1 - k >= z), TP - 1 - k > z, rup, rs_up),
+                (k, (z < TP - 1) & (k <= z), k < z, rdn, rs_dn),
+            ):
+                @pl.when(has)
+                def _():
+                    copy(dest, ch).wait_recv()
+
+                    @pl.when(onward)
+                    def _():
+                        part[dest, span] = (
+                            part[dest, span].astype(F32) + buf[dest, span].astype(F32)
+                        ).astype(BF16)
+                        copy(dest, ch).start()
+
+                    @pl.when(dest == z)
+                    def _():
+                        own[span] += buf[dest, span].astype(F32)
+
+        return carry
+
+    lax.fori_loop(0, TP, sum_step, 0)
+
+    squares = jnp.sum(own[...] * own[...], axis=1, keepdims=True)
+    as_row = jnp.sum(jnp.where(diagonal, squares, 0.0), axis=0, keepdims=True)
+    sq_mine[...] = jnp.broadcast_to(as_row, sq_mine.shape)
+
+    def sq_copy(d, slot):
+        return pltpu.make_async_remote_copy(
+            src_ref=sq_mine,
+            dst_ref=sq_all.at[slot],
+            send_sem=sq_send.at[d],
+            recv_sem=sq_recv.at[slot],
+            device_id={"tp": lax.rem(z + d, TP)},
+            device_id_type=MESH,
+        )
+
+    for d in range(1, TP):
+        sq_copy(d, z).start()
+    for d in range(1, TP):
+        slot = lax.rem(z + d, TP)
+        sq_copy(d, slot).wait_recv()
+        as_row = as_row + sq_all[slot, 0:1]
+    inv_post = lax.rsqrt(as_column(as_row) * (1.0 / model) + EPSILON)
+    out_ref[...] = (
+        tok_ref[...].astype(F32) + own[...] * inv_post * gain_post[z]
+    ).astype(BF16)
+
+    for d in range(1, TP):
+        sq_copy(d, z).wait_send()
+
+    def settle(i, carry):
+        for ch in range(CHUNKS):
+            @pl.when((z < TP - 1) & (i <= z))
+            def _():
+                ag_copy(xbuf.at[i, ch_rows[ch]], i, ch, ag_up, up).wait_send()
+
+            @pl.when((z > 0) & (i >= z))
+            def _():
+                ag_copy(xbuf.at[i, ch_rows[ch]], i, ch, ag_dn, down).wait_send()
+
+            @pl.when(i > z)
+            def _():
+                rs_up(i, ch).wait_send()
+
+            @pl.when(i < z)
+            def _():
+                rs_dn(i, ch).wait_send()
+
+        return carry
+
+    lax.fori_loop(0, TP, settle, 0)
+
+    @pl.when(c < CTX // 2)
+    def _():
+        kv_copy(c, 1, far).wait_send()
+
+    @pl.when(c % 2 == 0)
+    def _():
+        kv_copy(c, 0, partner).wait_send()
+
+    @pl.when(c >= CTX // 2)
+    def _():
+        kv_copy(c - 2, 2, partner).wait_send()
+
+
+def per_device_fused(
+    tokens, positions, first_key, input_gain, query_weight, kv_weight, query_gain, key_gain,
+    out_weight, post_gain,
+):
+    rows, feat = tokens.shape
+    hd = query_gain.shape[0]
+    q_cols = query_weight.shape[1]
+    kv_cols = kv_weight.shape[2]
+    model = query_weight.shape[0]
+    kv_heads = kv_cols // hd
+    vmem = pl.BlockSpec(memory_space=pltpu.VMEM)
+    anywhere = pl.BlockSpec(memory_space=pl.ANY)
+    dma = pltpu.SemaphoreType.DMA
+    state = (kv_heads, 2 * rows, hd)
+    return pl.pallas_call(
+        fused_kernel,
+        out_shape=jax.ShapeDtypeStruct((rows, feat), BF16),
+        in_specs=[vmem] * 7 + [anywhere] * 3,
+        out_specs=vmem,
+        scratch_shapes=[
+            pltpu.VMEM((TP, rows, feat), BF16),
+            pltpu.VMEM((rows, feat), BF16),
+            pltpu.VMEM((model, q_cols), BF16),
+            pltpu.VMEM((2, model, kv_cols), BF16),
+            pltpu.VMEM((q_cols, model), BF16),
+            pltpu.VMEM((TP, 1, feat), F32),
+            pltpu.VMEM((TP, 1, feat), F32),
+            pltpu.VMEM((rows, 1), F32),
+            pltpu.VMEM((rows, 2 * kv_cols), F32),
+            pltpu.VMEM((rows, q_cols), F32),
+            pltpu.VMEM((rows, hd), F32),
+            pltpu.VMEM((rows, hd), F32),
+            pltpu.VMEM((CTX, 2, rows, kv_cols), BF16),
+            pltpu.VMEM(state, BF16),
+            pltpu.VMEM((kv_heads, 2 * rows, 1), F32),
+            pltpu.VMEM((kv_heads, 2 * rows, 1), F32),
+            pltpu.VMEM(state, F32),
+            pltpu.VMEM((rows, q_cols), BF16),
+            pltpu.VMEM((TP, rows, feat), BF16),
+            pltpu.VMEM((TP, rows, feat), BF16),
+            pltpu.VMEM((TP, rows, feat), BF16),
+            pltpu.VMEM((rows, feat), F32),
+            pltpu.VMEM((8, rows), F32),
+            pltpu.VMEM((TP, 8, rows), F32),
+            dma((TP, 3)),
+            dma,
+            dma((TP, CHUNKS)),
+            dma((TP, CHUNKS)),
+            dma((TP, CHUNKS)),
+            dma((3,)),
+            dma((3,)),
+            dma((TP, CHUNKS)),
+            dma((TP, CHUNKS)),
+            dma((TP, CHUNKS)),
+            dma((TP, CHUNKS)),
+            dma((TP,)),
+            dma((TP,)),
+        ],
+        compiler_params=pltpu.CompilerParams(
+            collective_id=0, has_side_effects=True, vmem_limit_bytes=60 * 1024 * 1024
+        ),
+    )(
+        tokens,
+        positions.reshape(1, rows),
+        first_key.reshape(1, rows),
+        input_gain.reshape(1, model),
+        query_gain.reshape(1, hd),
+        key_gain.reshape(1, hd),
+        post_gain.reshape(1, model),
+        query_weight,
+        kv_weight,
+        out_weight,
+    )
+
+
 def solution(mesh):
+    fused = mesh.shape["tp"] == TP and mesh.shape["ctx"] == CTX
     return jax.shard_map(
-        per_device,
+        per_device_fused if fused else per_device,
         mesh=mesh,
         in_specs=(
             P(("group", "ctx"), "tp"),

time: 163 us -> 94.8 us (0.58); the launches traced: 161 us -> 94.4 us
  Pallas kernels: 0 us -> 88 us
  waiting for transfers between devices: 82.3 us -> 0 us
  matrix products: 23.8 us -> 0 us
  local copies, waits for them, and re-layouts: 27.9 us -> 6.47 us
  between operations: 13.7 us -> 0.01 us
  other arithmetic: 7.11 us -> 0 us
  starting transfers between devices: 5.98 us -> 0 us
    pallas_call x0 -> x1, Pallas kernels: none -> 88 us  [per_device_fused(): pl.pallas_call(fused_kernel, out_shape=jax.ShapeDtypeStruct((rows, feat),...]
    psum x1 -> x0, waiting for transfers between devices: 60.8 us -> none  [per_device(): lax.psum(partial_value.astype(jnp.bfloat16), 'tp').astype(jnp.float32)]
    dot_general x3 -> x0, local copies, waits for them, and re-layouts: 25.7 us -> none  [the longest x2 17.4 us: per_device(): key_raw = jnp.dot(normed, kv_full[0], preferred_element_type=jnp.float32)]
    dot_general x6 -> x0, matrix products: 23.8 us -> none  [the longest x1 9.61 us: per_device(): jnp.dot(attn, out_weight, preferred_element_type=jnp.float32)]
    ppermute x3 -> x0, waiting for transfers between devices: 10.5 us -> none  [passed_along(): return lax.ppermute(block, axis, route)]
    all_gather x1 -> x0, waiting for transfers between devices: 10.2 us -> none  [per_device(): lax.all_gather(tokens, 'tp', axis=1, tiled=True).astype(jnp.float32)]
    ppermute x3 -> x0, starting transfers between devices: 5.94 us -> none  [passed_along(): return lax.ppermute(block, axis, route)]
    reduce_sum x4 -> x0, other arithmetic: 4.82 us -> none  [the longest x3 4.44 us: rms_norm(): jnp.mean(values * values, axis=-1, keepdims=True) + EPSILON]
  transfers between devices with their start and end apart: 5 -> 0, of which waited for: 4 -> 0; matrix products, arithmetic and copies ran while one was open for 22% -> 0% of each run, Pallas kernels for 0% -> 0%
where the time goes in v1:
time: 94.8 us; the launch traced here: 94.4 us
  Pallas kernels  88 us (93%)
  local copies, waits for them, and re-layouts  6.47 us (7%)
    pallas_call x1, Pallas kernels, per_device_fused(): pl.pallas_call(fused_kernel, out_shape=jax.ShapeDtypeStruct((rows, feat),...  88 us

profile of v1, /device:TPU:2, one launch (start us, length us, event | category | flops | bytes accessed | tf_op | source)
XLA Modules:
  0.0 94.4 jit_solution(6011901654248307590)
XLA Ops:
  0.0 1.4 %reshape.20.ig_ref = f32[1,5376]{1,0:T(1,128)} reshape(f32[5376]{0:T(1024)} %param.13) | data formatting | bytes 43008 | tf_op jit(solution)/shard_map/reshape | solution.py:605
  1.4 1.4 %reshape.23.pg_ref = f32[1,5376]{1,0:T(1,128)} reshape(f32[5376]{0:T(1024)} %param.19) | data formatting | bytes 43008 | tf_op jit(solution)/shard_map/reshape | solution.py:608
  2.7 1.9 %copy.11.tok_ref = bf16[128,1344]{1,0:T(8,128)(2,1)} copy(bf16[128,1344]{0,1:T(8,128)(2,1)} %param.10) | data formatting | bytes 688128 | tf_op args[0]
  4.6 88.0 %shard_map.100 = bf16[128,1344]{1,0:T(8,128)(2,1)} custom-call(bf16[128,1344]{1,0:T(8,128)(2,1)} %copy.11.tok_ref, s32[1,128]{1,0:T(1,128)} %bitcast.4, s32[1,128]{1,0:T(1,128)} %bitcast.5, f32[1,5376]{1,0:T(1,128)} %reshape.20.ig_ref, f32[1,128]{1,0:T(1,128)} %bitcast.6, f32[1,128]{1,0:T(1,128)} %bitcast.7, f32[1,5376]{1,0:T(1,128)} %reshape.23.pg_ref, ...), custom_call_target="tpu_custom_call" | custom-call | tf_op jit(solution)/shard_map/pallas_call | solution.py:554
  92.6 1.9 %copy.12 = bf16[128,1344]{0,1:T(8,128)(2,1)} copy(bf16[128,1344]{1,0:T(8,128)(2,1)} %shard_map.100) | data formatting | bytes 688128 | tf_op jit(solution)/shard_map/pallas_call | solution.py:554

commit v2 on v1

--- a/solution.py
+++ b/solution.py
@@ -158,6 +158,13 @@
     crow = rows // CHUNKS
     ch_rows = [pl.ds(i * crow, crow) for i in range(CHUNKS)]
 
+    barrier = pltpu.get_barrier_semaphore()
+    for d in range(1, TP):
+        pl.semaphore_signal(
+            barrier, inc=1, device_id={"tp": lax.rem(z + d, TP)}, device_id_type=MESH
+        )
+    pl.semaphore_signal(barrier, inc=1, device_id={"ctx": partner}, device_id_type=MESH)
+    pl.semaphore_signal(barrier, inc=1, device_id={"ctx": far}, device_id_type=MESH)
     def weight_copies(src):
         span = pl.ds(pl.multiple_of(src * feat, 64), feat)
         return (
@@ -188,13 +195,6 @@
     wo_copy = pltpu.make_async_copy(ow_hbm, wo, wo_sem)
     wo_copy.start()
 
-    barrier = pltpu.get_barrier_semaphore()
-    for d in range(1, TP):
-        pl.semaphore_signal(
-            barrier, inc=1, device_id={"tp": lax.rem(z + d, TP)}, device_id_type=MESH
-        )
-    pl.semaphore_signal(barrier, inc=1, device_id={"ctx": partner}, device_id_type=MESH)
-    pl.semaphore_signal(barrier, inc=1, device_id={"ctx": far}, device_id_type=MESH)
     pl.semaphore_wait(barrier, TP + 1)
 
     up = {"tp": lax.rem(z + 1, TP)}
@@ -219,9 +219,11 @@
         def _():
             ag_copy(tok_ref.at[ch_rows[ch]], z, ch, ag_dn, down).start()
 
+    gains = ig_ref[...].reshape(1, model) * PRESCALE
+    post_gains = pg_ref[...].reshape(1, model)
     for i in range(TP):
-        gain_in[i] = ig_ref[:, i * feat : (i + 1) * feat] * PRESCALE
-        gain_post[i] = pg_ref[:, i * feat : (i + 1) * feat]
+        gain_in[i] = gains[:, i * feat : (i + 1) * feat]
+        gain_post[i] = post_gains[:, i * feat : (i + 1) * feat]
     xbuf[z] = tok_ref[...]
     ssq_ref[...] = jnp.zeros_like(ssq_ref)
     kv_acc[...] = jnp.zeros_like(kv_acc)
@@ -451,15 +453,17 @@
     def sum_step(k, carry):
         for ch in range(CHUNKS):
             span = ch_rows[ch]
-            for dest, has, onward, buf, copy in (
-                (TP - 1 - k, (z > 0) & (TP - 1 - k >= z), TP - 1 - k > z, rup, rs_up),
-                (k, (z < TP - 1) & (k <= z), k < z, rdn, rs_dn),
+            from_low = z + TP - 1 - k
+            from_high = z + k - (TP - 1)
+            for dest, has, buf, copy in (
+                (from_low, (z > 0) & (from_low < TP), rup, rs_up),
+                (from_high, (z < TP - 1) & (from_high >= 0), rdn, rs_dn),
             ):
                 @pl.when(has)
                 def _():
                     copy(dest, ch).wait_recv()
 
-                    @pl.when(onward)
+                    @pl.when(dest != z)
                     def _():
                         part[dest, span] = (
                             part[dest, span].astype(F32) + buf[dest, span].astype(F32)
@@ -472,7 +476,7 @@
 
         return carry
 
-    lax.fori_loop(0, TP, sum_step, 0)
+    lax.fori_loop(1, TP, sum_step, 0)
 
     squares = jnp.sum(own[...] * own[...], axis=1, keepdims=True)
     as_row = jnp.sum(jnp.where(diagonal, squares, 0.0), axis=0, keepdims=True)
@@ -602,10 +606,10 @@
         tokens,
         positions.reshape(1, rows),
         first_key.reshape(1, rows),
-        input_gain.reshape(1, model),
+        input_gain,
         query_gain.reshape(1, hd),
         key_gain.reshape(1, hd),
-        post_gain.reshape(1, model),
+        post_gain,
         query_weight,
         kv_weight,
         out_weight,

time: 94.8 us -> 73.8 us (0.78)
  Pallas kernels: 88 us -> 69.8 us
  local copies, waits for them, and re-layouts: 6.47 us -> 3.76 us
    pallas_call x1, Pallas kernels: 88 us -> 69.8 us  [per_device_fused(): pl.pallas_call(fused_kernel, out_shape=jax.ShapeDtypeStruct((rows, feat),...]
    reshape x2 -> x0, local copies, waits for them, and re-layouts: 2.71 us -> none  [the longest x1 1.36 us: per_device_fused(): input_gain.reshape(1, model)]
where the time goes in v2:
time: 73.8 us; the launch traced here: 73.6 us
  Pallas kernels  69.8 us (95%)
  local copies, waits for them, and re-layouts  3.76 us (5%)
    pallas_call x1, Pallas kernels, per_device_fused(): pl.pallas_call(fused_kernel, out_shape=jax.ShapeDtypeStruct((rows, feat),...  69.8 us
    pallas_call x1, local copies, waits for them, and re-layouts, per_device_fused(): pl.pallas_call(fused_kernel, out_shape=jax.ShapeDtypeStruct((rows, feat),...  1.89 us
    unnamed x1, local copies, waits for them, and re-layouts  1.88 us

profile of v2, /device:TPU:2, one launch (start us, length us, event | category | flops | bytes accessed | tf_op | source)
XLA Modules:
  0.0 73.6 jit_solution(6386955670558087905)
XLA Ops:
  0.0 1.9 %copy.11.tok_ref = bf16[128,1344]{1,0:T(8,128)(2,1)} copy(bf16[128,1344]{0,1:T(8,128)(2,1)} %param.10) | data formatting | bytes 688128 | tf_op args[0]
  1.9 69.8 %shard_map.100 = bf16[128,1344]{1,0:T(8,128)(2,1)} custom-call(bf16[128,1344]{1,0:T(8,128)(2,1)} %copy.11.tok_ref, s32[1,128]{1,0:T(1,128)} %bitcast.4, s32[1,128]{1,0:T(1,128)} %bitcast.5, f32[5376]{0:T(1024)} %ig_ref.1, f32[1,128]{1,0:T(1,128)} %bitcast.6, f32[1,128]{1,0:T(1,128)} %bitcast.7, f32[5376]{0:T(1024)} %pg_ref.1, bf16[5376,1024]{1,0:T(8,128)(2,1)} %qw_hbm.1, ...), custom_call_target="tpu_custom_call" | custom-call | tf_op jit(solution)/shard_map/pallas_call | solution.py:558
  71.7 1.9 %copy.12 = bf16[128,1344]{0,1:T(8,128)(2,1)} copy(bf16[128,1344]{1,0:T(8,128)(2,1)} %shard_map.100) | data formatting | bytes 688128 | tf_op jit(solution)/shard_map/pallas_call | solution.py:558

commit v3 on v2

--- a/solution.py
+++ b/solution.py
@@ -141,12 +141,13 @@
 
 def fused_kernel(
     tok_ref, pos_ref, fk_ref, ig_ref, qg_ref, kg_ref, pg_ref, qw_hbm, kvw_hbm, ow_hbm, out_ref,
-    xbuf, xg_ref, wq, wkv, wo, gain_in, gain_post, ssq_ref, kv_acc, q_acc, cos_ref, sin_ref,
+    xbuf, xg_ref, tok_rows, wq, wkv, wo, gain_in, gain_post, ssq_ref, kv_acc, q_acc, cos_ref, sin_ref,
     kvbuf, q_ref, m_ref, l_ref, o_ref, attn_ref, part, rup, rdn, own, sq_mine, sq_all,
     w_sem, wo_sem, ag_up, ag_dn, ag_recv, kv_send, kv_recv,
     rs_up_send, rs_dn_send, rs_up_recv, rs_dn_recv, sq_send, sq_recv,
 ):
-    rows, feat = tok_ref.shape
+    feat, rows = tok_ref.shape
+    piece = feat // CHUNKS
     hd = qg_ref.shape[1]
     kv_heads = wkv.shape[2] // hd
     heads = wq.shape[1] // hd
@@ -165,12 +166,15 @@
         )
     pl.semaphore_signal(barrier, inc=1, device_id={"ctx": partner}, device_id_type=MESH)
     pl.semaphore_signal(barrier, inc=1, device_id={"ctx": far}, device_id_type=MESH)
-    def weight_copies(src):
-        span = pl.ds(pl.multiple_of(src * feat, 64), feat)
+    def weight_span(src, ch):
+        return pl.ds(pl.multiple_of(src * feat + ch * piece, 32), piece)
+
+    def weight_copies(src, ch):
+        span = weight_span(src, ch)
         return (
-            pltpu.make_async_copy(kvw_hbm.at[0, span], wkv.at[0, span], w_sem.at[src, 0]),
-            pltpu.make_async_copy(kvw_hbm.at[1, span], wkv.at[1, span], w_sem.at[src, 1]),
-            pltpu.make_async_copy(qw_hbm.at[span], wq.at[span], w_sem.at[src, 2]),
+            pltpu.make_async_copy(kvw_hbm.at[0, span], wkv.at[0, span], w_sem.at[src, ch, 0]),
+            pltpu.make_async_copy(kvw_hbm.at[1, span], wkv.at[1, span], w_sem.at[src, ch, 1]),
+            pltpu.make_async_copy(qw_hbm.at[span], wq.at[span], w_sem.at[src, ch, 2]),
         )
 
     def each_source(fn):
@@ -188,8 +192,9 @@
         lax.fori_loop(0, TP, at_distance, 0)
 
     def begin_weights(src, d):
-        for copy in weight_copies(src):
-            copy.start()
+        for ch in range(CHUNKS):
+            for copy in weight_copies(src, ch):
+                copy.start()
 
     each_source(begin_weights)
     wo_copy = pltpu.make_async_copy(ow_hbm, wo, wo_sem)
@@ -200,10 +205,13 @@
     up = {"tp": lax.rem(z + 1, TP)}
     down = {"tp": lax.rem(z + TP - 1, TP)}
 
+    def piece_of(ch):
+        return pl.ds(pl.multiple_of(ch * piece, 32), piece)
+
     def ag_copy(source, src, ch, send, target):
         return pltpu.make_async_remote_copy(
             src_ref=source,
-            dst_ref=xbuf.at[src, ch_rows[ch]],
+            dst_ref=xbuf.at[src, piece_of(ch)],
             send_sem=send.at[src, ch],
             recv_sem=ag_recv.at[src, ch],
             device_id=target,
@@ -213,16 +221,17 @@
     for ch in range(CHUNKS):
         @pl.when(z < TP - 1)
         def _():
-            ag_copy(tok_ref.at[ch_rows[ch]], z, ch, ag_up, up).start()
+            ag_copy(tok_ref.at[piece_of(ch)], z, ch, ag_up, up).start()
 
         @pl.when(z > 0)
         def _():
-            ag_copy(tok_ref.at[ch_rows[ch]], z, ch, ag_dn, down).start()
+            ag_copy(tok_ref.at[piece_of(ch)], z, ch, ag_dn, down).start()
 
     gains = ig_ref[...].reshape(1, model) * PRESCALE
     post_gains = pg_ref[...].reshape(1, model)
+    for i in range(TP * CHUNKS):
+        gain_in[i] = gains[:, i * piece : (i + 1) * piece]
     for i in range(TP):
-        gain_in[i] = gains[:, i * feat : (i + 1) * feat]
         gain_post[i] = post_gains[:, i * feat : (i + 1) * feat]
     xbuf[z] = tok_ref[...]
     ssq_ref[...] = jnp.zeros_like(ssq_ref)
@@ -245,64 +254,66 @@
 
     last = jnp.where(z < TP // 2, TP - 1, 0)
 
-    def query_product(src):
-        span = pl.ds(pl.multiple_of(src * feat, 64), feat)
-        weight_copies(src)[2].wait()
-        q_acc[...] += jnp.dot(xg_ref[...], wq[span], preferred_element_type=F32)
-
-    def projections(src):
-        x = xbuf[src].astype(F32)
-        ssq_ref[...] += jnp.sum(x * x, axis=1, keepdims=True)
-        xg_ref[...] = (x * gain_in[src]).astype(BF16)
-        span = pl.ds(pl.multiple_of(src * feat, 64), feat)
+    def query_product(src, ch):
+        weight_copies(src, ch)[2].wait()
+        q_acc[...] += jnp.dot(
+            xg_ref[...], wq[weight_span(src, ch)], preferred_element_type=F32
+        )
+
+    def projections(src, ch):
+        x_t = xbuf[src, piece_of(ch)].astype(F32)
+        ssq_ref[...] += jnp.sum(x_t * x_t, axis=0, keepdims=True)
+        xg_ref[...] = (x_t.T * gain_in[src * CHUNKS + ch]).astype(BF16)
         width = wkv.shape[2]
         for i in range(2):
-            weight_copies(src)[i].wait()
+            weight_copies(src, ch)[i].wait()
             kv_acc[:, i * width : (i + 1) * width] += jnp.dot(
-                xg_ref[...], wkv[i, span], preferred_element_type=F32
+                xg_ref[...], wkv[i, weight_span(src, ch)], preferred_element_type=F32
             )
 
-        @pl.when(src != last)
-        def _():
-            query_product(src)
-
-    def at_distance(d, carry):
+        @pl.when((src != last) | (ch < CHUNKS - 1))
+        def _():
+            query_product(src, ch)
+
+    def gather_step(k, carry):
+        d = k // CHUNKS
+        ch = k % CHUNKS
         low = z - d
         high = z + d
-        for ch in range(CHUNKS):
-            @pl.when((d > 0) & (low >= 0))
-            def _():
-                here = xbuf.at[low, ch_rows[ch]]
-                ag_copy(here, low, ch, ag_up, down).wait_recv()
-
-                @pl.when(z < TP - 1)
-                def _():
-                    ag_copy(here, low, ch, ag_up, up).start()
-
-            @pl.when((d > 0) & (high < TP))
-            def _():
-                here = xbuf.at[high, ch_rows[ch]]
-                ag_copy(here, high, ch, ag_dn, up).wait_recv()
-
-                @pl.when(z > 0)
-                def _():
-                    ag_copy(here, high, ch, ag_dn, down).start()
+
+        @pl.when((d > 0) & (low >= 0))
+        def _():
+            here = xbuf.at[low, piece_of(ch)]
+            ag_copy(here, low, ch, ag_up, down).wait_recv()
+
+            @pl.when(z < TP - 1)
+            def _():
+                ag_copy(here, low, ch, ag_up, up).start()
+
+        @pl.when((d > 0) & (high < TP))
+        def _():
+            here = xbuf.at[high, piece_of(ch)]
+            ag_copy(here, high, ch, ag_dn, up).wait_recv()
+
+            @pl.when(z > 0)
+            def _():
+                ag_copy(here, high, ch, ag_dn, down).start()
 
         def side(i, inner):
             src = jnp.where(i == 0, low, high)
 
             @pl.when((src >= 0) & (src < TP) & ((d > 0) | (i == 0)))
             def _():
-                projections(src)
+                projections(src, ch)
 
             return inner
 
         lax.fori_loop(0, 2, side, 0)
         return carry
 
-    lax.fori_loop(0, TP, at_distance, 0)
-
-    inv = lax.rsqrt(ssq_ref[...] * (1.0 / model) + EPSILON) * (1.0 / PRESCALE)
+    lax.fori_loop(0, TP * CHUNKS, gather_step, 0)
+
+    inv = lax.rsqrt(as_column(ssq_ref[...]) * (1.0 / model) + EPSILON) * (1.0 / PRESCALE)
 
     def normed_rotated(raw, gain_vec):
         raw = raw * inv
@@ -333,7 +344,7 @@
     def _():
         kv_copy(c, 0, partner).start()
 
-    query_product(last)
+    query_product(last, CHUNKS - 1)
     for h in range(heads):
         cols = slice(h * hd, (h + 1) * hd)
         spot = slice((h % 2) * rows, (h % 2 + 1) * rows)
@@ -449,6 +460,7 @@
 
     lax.fori_loop(0, TP, out_step, 0)
     own[...] = part[z].astype(F32)
+    tok_rows[...] = tok_ref[...].astype(F32).T
 
     def sum_step(k, carry):
         for ch in range(CHUNKS):
@@ -500,7 +512,7 @@
         as_row = as_row + sq_all[slot, 0:1]
     inv_post = lax.rsqrt(as_column(as_row) * (1.0 / model) + EPSILON)
     out_ref[...] = (
-        tok_ref[...].astype(F32) + own[...] * inv_post * gain_post[z]
+        tok_rows[...] + own[...] * inv_post * gain_post[z]
     ).astype(BF16)
 
     for d in range(1, TP):
@@ -510,11 +522,11 @@
         for ch in range(CHUNKS):
             @pl.when((z < TP - 1) & (i <= z))
             def _():
-                ag_copy(xbuf.at[i, ch_rows[ch]], i, ch, ag_up, up).wait_send()
+                ag_copy(xbuf.at[i, piece_of(ch)], i, ch, ag_up, up).wait_send()
 
             @pl.when((z > 0) & (i >= z))
             def _():
-                ag_copy(xbuf.at[i, ch_rows[ch]], i, ch, ag_dn, down).wait_send()
+                ag_copy(xbuf.at[i, piece_of(ch)], i, ch, ag_dn, down).wait_send()
 
             @pl.when(i > z)
             def _():
@@ -545,7 +557,8 @@
     tokens, positions, first_key, input_gain, query_weight, kv_weight, query_gain, key_gain,
     out_weight, post_gain,
 ):
-    rows, feat = tokens.shape
+    feat, rows = tokens.shape[1], tokens.shape[0]
+    piece = feat // CHUNKS
     hd = query_gain.shape[0]
     q_cols = query_weight.shape[1]
     kv_cols = kv_weight.shape[2]
@@ -561,14 +574,15 @@
         in_specs=[vmem] * 7 + [anywhere] * 3,
         out_specs=vmem,
         scratch_shapes=[
-            pltpu.VMEM((TP, rows, feat), BF16),
-            pltpu.VMEM((rows, feat), BF16),
+            pltpu.VMEM((TP, feat, rows), BF16),
+            pltpu.VMEM((rows, piece), BF16),
+            pltpu.VMEM((rows, feat), F32),
             pltpu.VMEM((model, q_cols), BF16),
             pltpu.VMEM((2, model, kv_cols), BF16),
             pltpu.VMEM((q_cols, model), BF16),
+            pltpu.VMEM((TP * CHUNKS, 1, piece), F32),
             pltpu.VMEM((TP, 1, feat), F32),
-            pltpu.VMEM((TP, 1, feat), F32),
-            pltpu.VMEM((rows, 1), F32),
+            pltpu.VMEM((1, rows), F32),
             pltpu.VMEM((rows, 2 * kv_cols), F32),
             pltpu.VMEM((rows, q_cols), F32),
             pltpu.VMEM((rows, hd), F32),
@@ -585,7 +599,7 @@
             pltpu.VMEM((rows, feat), F32),
             pltpu.VMEM((8, rows), F32),
             pltpu.VMEM((TP, 8, rows), F32),
-            dma((TP, 3)),
+            dma((TP, CHUNKS, 3)),
             dma,
             dma((TP, CHUNKS)),
             dma((TP, CHUNKS)),
@@ -603,7 +617,7 @@
             collective_id=0, has_side_effects=True, vmem_limit_bytes=60 * 1024 * 1024
         ),
     )(
-        tokens,
+        tokens.T,
         positions.reshape(1, rows),
         first_key.reshape(1, rows),
         input_gain,

time: 73.8 us -> 70.6 us (0.957)
  local copies, waits for them, and re-layouts: 3.76 us -> 1.89 us
  Pallas kernels: 69.8 us -> 68.5 us
    unnamed x1 -> x0, local copies, waits for them, and re-layouts: 1.88 us -> none
    pallas_call x1, Pallas kernels: 69.8 us -> 68.5 us  [per_device_fused(): pl.pallas_call(fused_kernel, out_shape=jax.ShapeDtypeStruct((rows, feat),...]
where the time goes in v3:
time: 70.6 us; the launch traced here: 70.4 us
  Pallas kernels  68.5 us (97%)
  local copies, waits for them, and re-layouts  1.89 us (3%)
    pallas_call x1, Pallas kernels, per_device_fused(): pl.pallas_call(fused_kernel, out_shape=jax.ShapeDtypeStruct((rows, feat),...  68.5 us
    pallas_call x1, local copies, waits for them, and re-layouts, per_device_fused(): pl.pallas_call(fused_kernel, out_shape=jax.ShapeDtypeStruct((rows, feat),...  1.89 us

profile of v3, /device:TPU:2, one launch (start us, length us, event | category | flops | bytes accessed | tf_op | source)
XLA Modules:
  0.0 70.4 jit_solution(17285548463951211409)
XLA Ops:
  0.0 68.5 %shard_map.100 = bf16[128,1344]{1,0:T(8,128)(2,1)} custom-call(bf16[1344,128]{1,0:T(8,128)(2,1)} %bitcast.5, s32[1,128]{1,0:T(1,128)} %bitcast.6, s32[1,128]{1,0:T(1,128)} %bitcast.7, f32[5376]{0:T(1024)} %ig_ref.1, f32[1,128]{1,0:T(1,128)} %bitcast.8, f32[1,128]{1,0:T(1,128)} %bitcast.9, f32[5376]{0:T(1024)} %pg_ref.1, bf16[5376,1024]{1,0:T(8,128)(2,1)} %qw_hbm.1, ...), custom_call_target="tpu_custom_call" | custom-call | tf_op jit(solution)/shard_map/pallas_call | solution.py:571
  68.5 1.9 %copy.11 = bf16[128,1344]{0,1:T(8,128)(2,1)} copy(bf16[128,1344]{1,0:T(8,128)(2,1)} %shard_map.100) | data formatting | bytes 688128 | tf_op jit(solution)/shard_map/pallas_call | solution.py:571

commit v4 on v3

--- a/solution.py
+++ b/solution.py
@@ -141,7 +141,7 @@
 
 def fused_kernel(
     tok_ref, pos_ref, fk_ref, ig_ref, qg_ref, kg_ref, pg_ref, qw_hbm, kvw_hbm, ow_hbm, out_ref,
-    xbuf, xg_ref, tok_rows, wq, wkv, wo, gain_in, gain_post, ssq_ref, kv_acc, q_acc, cos_ref, sin_ref,
+    xbuf, xg_ref, gain_out, wq, wkv, wo, gain_in, gain_post, ssq_ref, kv_acc, q_acc, cos_ref, sin_ref,
     kvbuf, q_ref, m_ref, l_ref, o_ref, attn_ref, part, rup, rdn, own, sq_mine, sq_all,
     w_sem, wo_sem, ag_up, ag_dn, ag_recv, kv_send, kv_recv,
     rs_up_send, rs_dn_send, rs_up_recv, rs_dn_recv, sq_send, sq_recv,
@@ -156,14 +156,19 @@
     c = lax.axis_index("ctx")
     partner = c + 1 - 2 * (c % 2)
     far = lax.rem(c + 2, CTX)
-    crow = rows // CHUNKS
-    ch_rows = [pl.ds(i * crow, crow) for i in range(CHUNKS)]
 
     barrier = pltpu.get_barrier_semaphore()
-    for d in range(1, TP):
-        pl.semaphore_signal(
-            barrier, inc=1, device_id={"tp": lax.rem(z + d, TP)}, device_id_type=MESH
-        )
+    up = {"tp": lax.rem(z + 1, TP)}
+    down = {"tp": lax.rem(z + TP - 1, TP)}
+
+    @pl.when(z < TP - 1)
+    def _():
+        pl.semaphore_signal(barrier, inc=1, device_id=up, device_id_type=MESH)
+
+    @pl.when(z > 0)
+    def _():
+        pl.semaphore_signal(barrier, inc=1, device_id=down, device_id_type=MESH)
+
     pl.semaphore_signal(barrier, inc=1, device_id={"ctx": partner}, device_id_type=MESH)
     pl.semaphore_signal(barrier, inc=1, device_id={"ctx": far}, device_id_type=MESH)
     def weight_span(src, ch):
@@ -200,10 +205,7 @@
     wo_copy = pltpu.make_async_copy(ow_hbm, wo, wo_sem)
     wo_copy.start()
 
-    pl.semaphore_wait(barrier, TP + 1)
-
-    up = {"tp": lax.rem(z + 1, TP)}
-    down = {"tp": lax.rem(z + TP - 1, TP)}
+    pl.semaphore_wait(barrier, jnp.where((z > 0) & (z < TP - 1), 4, 3))
 
     def piece_of(ch):
         return pl.ds(pl.multiple_of(ch * piece, 32), piece)
@@ -250,6 +252,7 @@
     cos_ref[...] = jnp.cos(angles)
     sines = jnp.sin(angles)
     sin_ref[...] = jnp.where(lane < hd // 2, -sines, sines)
+    gain_out[...] = jnp.broadcast_to(gain_post[z], (rows, feat)).T
     first = as_column(fk_ref[...].astype(F32)).astype(jnp.int32)
 
     last = jnp.where(z < TP // 2, TP - 1, 0)
@@ -410,8 +413,8 @@
 
     def rs_copy(dest, ch, buf, send, recv, target):
         return pltpu.make_async_remote_copy(
-            src_ref=part.at[dest, ch_rows[ch]],
-            dst_ref=buf.at[dest, ch_rows[ch]],
+            src_ref=part.at[dest, piece_of(ch)],
+            dst_ref=buf.at[dest, piece_of(ch)],
             send_sem=send.at[dest, ch],
             recv_sem=recv.at[dest, ch],
             device_id=target,
@@ -437,15 +440,15 @@
         start = pl.multiple_of((dest // 2) * (2 * feat) + odd * (feat - shift), 128)
         term = jnp.dot(
             attn_ref[...], wo[:, pl.ds(start, wide)], preferred_element_type=F32
-        ).astype(BF16)
+        ).T.astype(BF16)
 
         @pl.when(odd == 0)
         def _():
-            part[dest] = term[:, :feat]
+            part[dest] = term[:feat]
 
         @pl.when(odd == 1)
         def _():
-            part[dest] = term[:, shift:]
+            part[dest] = term[shift:]
 
         for ch in range(CHUNKS):
             @pl.when((z == 0) & (dest > 0))
@@ -460,11 +463,10 @@
 
     lax.fori_loop(0, TP, out_step, 0)
     own[...] = part[z].astype(F32)
-    tok_rows[...] = tok_ref[...].astype(F32).T
 
     def sum_step(k, carry):
         for ch in range(CHUNKS):
-            span = ch_rows[ch]
+            span = piece_of(ch)
             from_low = z + TP - 1 - k
             from_high = z + k - (TP - 1)
             for dest, has, buf, copy in (
@@ -490,8 +492,7 @@
 
     lax.fori_loop(1, TP, sum_step, 0)
 
-    squares = jnp.sum(own[...] * own[...], axis=1, keepdims=True)
-    as_row = jnp.sum(jnp.where(diagonal, squares, 0.0), axis=0, keepdims=True)
+    as_row = jnp.sum(own[...] * own[...], axis=0, keepdims=True)
     sq_mine[...] = jnp.broadcast_to(as_row, sq_mine.shape)
 
     def sq_copy(d, slot):
@@ -510,9 +511,9 @@
         slot = lax.rem(z + d, TP)
         sq_copy(d, slot).wait_recv()
         as_row = as_row + sq_all[slot, 0:1]
-    inv_post = lax.rsqrt(as_column(as_row) * (1.0 / model) + EPSILON)
+    inv_post = lax.rsqrt(as_row * (1.0 / model) + EPSILON)
     out_ref[...] = (
-        tok_rows[...] + own[...] * inv_post * gain_post[z]
+        tok_ref[...].astype(F32) + own[...] * inv_post * gain_out[...]
     ).astype(BF16)
 
     for d in range(1, TP):
@@ -570,13 +571,13 @@
     state = (kv_heads, 2 * rows, hd)
     return pl.pallas_call(
         fused_kernel,
-        out_shape=jax.ShapeDtypeStruct((rows, feat), BF16),
+        out_shape=jax.ShapeDtypeStruct((feat, rows), BF16),
         in_specs=[vmem] * 7 + [anywhere] * 3,
         out_specs=vmem,
         scratch_shapes=[
             pltpu.VMEM((TP, feat, rows), BF16),
             pltpu.VMEM((rows, piece), BF16),
-            pltpu.VMEM((rows, feat), F32),
+            pltpu.VMEM((feat, rows), F32),
             pltpu.VMEM((model, q_cols), BF16),
             pltpu.VMEM((2, model, kv_cols), BF16),
             pltpu.VMEM((q_cols, model), BF16),
@@ -593,10 +594,10 @@
             pltpu.VMEM((kv_heads, 2 * rows, 1), F32),
             pltpu.VMEM(state, F32),
             pltpu.VMEM((rows, q_cols), BF16),
-            pltpu.VMEM((TP, rows, feat), BF16),
-            pltpu.VMEM((TP, rows, feat), BF16),
-            pltpu.VMEM((TP, rows, feat), BF16),
-            pltpu.VMEM((rows, feat), F32),
+            pltpu.VMEM((TP, feat, rows), BF16),
+            pltpu.VMEM((TP, feat, rows), BF16),
+            pltpu.VMEM((TP, feat, rows), BF16),
+            pltpu.VMEM((feat, rows), F32),
             pltpu.VMEM((8, rows), F32),
             pltpu.VMEM((TP, 8, rows), F32),
             dma((TP, CHUNKS, 3)),
@@ -627,7 +628,7 @@
         query_weight,
         kv_weight,
         out_weight,
-    )
+    ).T
 
 
 def solution(mesh):

time: 70.6 us -> 69.2 us (0.980)
  Pallas kernels: 68.5 us -> 67.3 us
    pallas_call x1 -> x0, local copies, waits for them, and re-layouts: 1.89 us -> none  [per_device_fused(): pl.pallas_call(fused_kernel, out_shape=jax.ShapeDtypeStruct((rows, feat),...]
    unnamed x0 -> x1, local copies, waits for them, and re-layouts: none -> 1.73 us
    pallas_call x1, Pallas kernels: 68.5 us -> 67.3 us  [per_device_fused(): pl.pallas_call(fused_kernel, out_shape=jax.ShapeDtypeStruct((feat, rows),...]
where the time goes in v4:
time: 69.2 us; the launch traced here: 69.1 us
  Pallas kernels  67.3 us (97%)
  local copies, waits for them, and re-layouts  1.73 us (2%)
    pallas_call x1, Pallas kernels, per_device_fused(): pl.pallas_call(fused_kernel, out_shape=jax.ShapeDtypeStruct((feat, rows),...  67.3 us
    unnamed x1, local copies, waits for them, and re-layouts  1.73 us

profile of v4, /device:TPU:2, one launch (start us, length us, event | category | flops | bytes accessed | tf_op | source)
XLA Modules:
  0.0 69.1 jit_solution(5970378994075917195)
XLA Ops:
  0.0 67.3 %shard_map.100 = bf16[1344,128]{1,0:T(8,128)(2,1)} custom-call(bf16[1344,128]{1,0:T(8,128)(2,1)} %bitcast.7, s32[1,128]{1,0:T(1,128)} %bitcast.8, s32[1,128]{1,0:T(1,128)} %bitcast.9, f32[5376]{0:T(1024)} %ig_ref.1, f32[1,128]{1,0:T(1,128)} %bitcast.10, f32[1,128]{1,0:T(1,128)} %bitcast.11, f32[5376]{0:T(1024)} %pg_ref.1, bf16[5376,1024]{1,0:T(8,128)(2,1)} %qw_hbm.1, ...), custom_call_target="tpu_custom_call" | custom-call | tf_op jit(solution)/shard_map/pallas_call | solution.py:572
  67.3 1.7 %copy.12 = bf16[128,1344]{0,1:T(8,128)(2,1)} copy(bf16[128,1344]{0,1:T(8,128)(2,1)} %bitcast.6) | data formatting | bytes 688128

commit v5 on v4

--- a/solution.py
+++ b/solution.py
@@ -427,41 +427,40 @@
     def rs_dn(dest, ch):
         return rs_copy(dest, ch, rdn, rs_dn_send, rs_dn_recv, down)
 
-    shift = feat % 128
-    wide = feat + shift
-
-    def out_step(k, carry):
+    extra = piece % 128
+    turns = 128 // extra
+    wide = piece + 128 - extra
+
+    def out_step(step, carry):
+        k = step // CHUNKS
+        ch = step % CHUNKS
         outer = TP - 1 - k
         inner = jnp.where(k == 0, 3, jnp.where(k == 1, 0, jnp.where(k == 2, 2, 1)))
         edge = (z == 0) | (z == TP - 1)
         dest = jnp.where(edge, outer, inner)
         dest = jnp.where(z < TP // 2, dest, TP - 1 - dest)
-        odd = dest % 2
-        start = pl.multiple_of((dest // 2) * (2 * feat) + odd * (feat - shift), 128)
+        spot = dest * CHUNKS + ch
+        turn = spot % turns
+        start = pl.multiple_of(spot * piece - turn * extra, 128)
         term = jnp.dot(
             attn_ref[...], wo[:, pl.ds(start, wide)], preferred_element_type=F32
         ).T.astype(BF16)
-
-        @pl.when(odd == 0)
-        def _():
-            part[dest] = term[:feat]
-
-        @pl.when(odd == 1)
-        def _():
-            part[dest] = term[shift:]
-
-        for ch in range(CHUNKS):
-            @pl.when((z == 0) & (dest > 0))
-            def _():
-                rs_up(dest, ch).start()
-
-            @pl.when((z == TP - 1) & (dest < TP - 1))
-            def _():
-                rs_dn(dest, ch).start()
+        for i in range(turns):
+            @pl.when(turn == i)
+            def _():
+                part[dest, piece_of(ch)] = term[i * extra : i * extra + piece]
+
+        @pl.when((z == 0) & (dest > 0))
+        def _():
+            rs_up(dest, ch).start()
+
+        @pl.when((z == TP - 1) & (dest < TP - 1))
+        def _():
+            rs_dn(dest, ch).start()
 
         return carry
 
-    lax.fori_loop(0, TP, out_step, 0)
+    lax.fori_loop(0, TP * CHUNKS, out_step, 0)
     own[...] = part[z].astype(F32)
 
     def sum_step(k, carry):

time: 69.2 us -> 69 us (level)
  no operation moved by 1% of the time
where the time goes in v5:
time: 69 us; the launch traced here: 68.9 us
  Pallas kernels  67.1 us (97%)
  local copies, waits for them, and re-layouts  1.73 us (3%)
    pallas_call x1, Pallas kernels, per_device_fused(): pl.pallas_call(fused_kernel, out_shape=jax.ShapeDtypeStruct((feat, rows),...  67.1 us
    unnamed x1, local copies, waits for them, and re-layouts  1.73 us

profile of v5, /device:TPU:2, one launch (start us, length us, event | category | flops | bytes accessed | tf_op | source)
XLA Modules:
  0.0 68.9 jit_solution(5527488999925668976)
XLA Ops:
  0.0 67.1 %shard_map.100 = bf16[1344,128]{1,0:T(8,128)(2,1)} custom-call(bf16[1344,128]{1,0:T(8,128)(2,1)} %bitcast.7, s32[1,128]{1,0:T(1,128)} %bitcast.8, s32[1,128]{1,0:T(1,128)} %bitcast.9, f32[5376]{0:T(1024)} %ig_ref.1, f32[1,128]{1,0:T(1,128)} %bitcast.10, f32[1,128]{1,0:T(1,128)} %bitcast.11, f32[5376]{0:T(1024)} %pg_ref.1, bf16[5376,1024]{1,0:T(8,128)(2,1)} %qw_hbm.1, ...), custom_call_target="tpu_custom_call" | custom-call | tf_op jit(solution)/shard_map/pallas_call | solution.py:571
  67.1 1.7 %copy.12 = bf16[128,1344]{0,1:T(8,128)(2,1)} copy(bf16[128,1344]{0,1:T(8,128)(2,1)} %bitcast.6) | data formatting | bytes 688128
